TPU v7x, 32 devices: a whole 2x2x4 slice. The times are simulated.
32 devices in a mesh: tm: 8 (over z, y), order: 4 (over x, core).
Axes of the slice: x: 2, y: 2, z: 4, core: 2. Of those that a mesh axis runs over, the one named last changes fastest.
Arguments:
- longitude: float32 [32768], P('tm'), may hold values from -3.140625 to 3.140625
- node_index: int32 [32768], P('tm'), may hold values from 0 to 159
- weight: float32 [32768], P('tm'), may hold values from 0.5 to 2
- gradient: float32 [32768], P('tm'), may hold values from 2 to 6
- segment: int32 [32768], P('tm'), may hold values from 0 to 31, never falling along the last dimension, each value on 1 to 4096 neighbouring positions
- order_map: int32 [304], P('order'), may hold values from 0 to 303, each once
- legendre: bfloat16 [304, 160, 304], P('order'), may hold values from -0.0625 to 0.0625
- precond: float32 [19, 2, 304, 304], P(None, None, 'order'), may hold values from 0 to 1, as said below
- kaula_prior: float32 [2, 304, 304], P(None, 'order'), may hold values from 0.5 to 5
- start_iterate: float32 [2, 304, 304], P(None, 'order'), may hold values from -6 to 6
- direction: float32 [2, 304, 304], P(None, 'order'), may hold values from -6 to 6
Outputs:
- iterate: float32 [2, 304, 304], P(None, 'order')
- residual: float32 [2, 304, 304], P(None, 'order')
- new_direction: float32 [2, 304, 304], P(None, 'order')
Inputs may be any that keep to these rules, and one draw needn't show every extreme that they name: `precond`: each block of 19 degrees is a symmetric positive definite matrix.
All inputs are finite; a program needn't handle non-finite values.
Results may differ from a plain program's by a relative error of at most 0.0003.
Values sent between devices are 32-bit elements; how exact they have to be, the bound alone decides.
No kernel may reach another device: no remote copies, remote signals or barrier semaphores. Data moves between devices by JAX's collectives and lax.ppermute only.
A program may use at most 128 MiB of HBM per device.

v0:
```python
import jax
import jax.numpy as jnp
from jax import lax
from jax.sharding import PartitionSpec as P

LMAX = 300
DB = 19
ITERS = 2


def extended(x, sides, width):
    for axis, dim in sides:
        size, length = (lax.axis_size(axis), x.shape[dim])
        up = [(i, (i + 1) % size) for i in range(size - 1)]
        down = [(j, i) for i, j in up]
        last = lax.slice_in_dim(x, length - width, length, axis=dim)
        leading = lax.slice_in_dim(x, 0, width, axis=dim)
        before = lax.ppermute(last, axis, up)
        after = lax.ppermute(leading, axis, down)
        x = jnp.concatenate([before, x, after], axis=dim)
    return x


def valid_mask_of(order_map, degrees):
    order_ids = order_map[None, :, None]
    degree_ids = jnp.arange(degrees, dtype=jnp.int32)[None, None, :]
    part_ids = jnp.arange(2, dtype=jnp.int32)[:, None, None]
    keep = (
        (degree_ids <= LMAX)
        & (degree_ids >= jnp.maximum(order_ids, 2))
        & ((part_ids == 0) | (order_ids >= 1))
    )
    return keep.astype(jnp.float32)


def make_phase(longitude, order_map):
    angle = longitude[:, None] * order_map.astype(jnp.float32)[None, :]
    return jnp.concatenate([jnp.cos(angle), jnp.sin(angle)], axis=1)


def precondition(blocks, vector):
    flat = vector.reshape(-1)
    block_count = flat.shape[0] // DB
    shaped = blocks.reshape(DB, block_count, DB)
    result = jnp.einsum(
        "jbi,bj->bi", shaped, flat.reshape(block_count, DB), precision=lax.Precision.HIGHEST
    )
    return result.reshape(vector.shape)


def run_steps(
    residual,
    iterate,
    new_direction,
    valid_mask,
    kaula_prior,
    precond,
    image_sum,
    pair_sum,
    single_sum,
):
    for iteration in range(ITERS):
        image = valid_mask * (kaula_prior * new_direction - image_sum(new_direction))
        residual_dot, curvature = pair_sum(
            jnp.sum(residual * new_direction), jnp.sum(new_direction * image)
        )
        step_size = residual_dot / curvature
        iterate = iterate + step_size * new_direction
        residual = residual - step_size * image
        smoothed = valid_mask * precondition(precond, residual)
        conj_dot = single_sum(jnp.sum(smoothed * image))
        new_direction = smoothed - conj_dot / curvature * new_direction
    return (iterate, residual, new_direction)


def shards(
    longitude,
    node_index,
    weight,
    gradient,
    segment,
    order_map,
    legendre,
    precond,
    kaula_prior,
    start_iterate,
    direction,
):
    row_count = longitude.shape[0]
    slot_count, node_count, degrees = legendre.shape
    valid_mask = valid_mask_of(order_map, degrees)
    selector = (jnp.arange(node_count, dtype=jnp.int32)[:, None] == node_index[None, :]).astype(
        jnp.float32
    )
    first_id = segment[0]
    last_id = segment[-1]
    offset = segment - first_id
    tail_index = last_id - first_id
    weight_sums = jax.ops.segment_sum(weight, offset, num_segments=row_count)
    edge_stats = jnp.stack(
        [
            jnp.stack([first_id, last_id]).astype(jnp.float32) + 1.0,
            jnp.stack([weight_sums[0], weight_sums[tail_index]]),
        ]
    )
    padded = extended(edge_stats, (("tm", 1),), 1)
    join_prev = (padded[0, 0] == edge_stats[0, 0]).astype(jnp.float32)
    join_next = (padded[0, 3] == edge_stats[0, 1]).astype(jnp.float32)
    weight_sums = (
        weight_sums.at[0].add(join_prev * padded[1, 0]).at[tail_index].add(join_next * padded[1, 3])
    )
    weight_sums = jnp.where(weight_sums > 0.0, weight_sums, 1.0)

    def center_rows(values):
        value_sums = jax.ops.segment_sum(weight * values, offset, num_segments=row_count)
        edge_sums = jnp.stack([value_sums[0], value_sums[tail_index]])
        beside_all = extended(edge_sums, (("tm", 0),), 1)
        value_sums = (
            value_sums.at[0]
            .add(join_prev * beside_all[0])
            .at[tail_index]
            .add(join_next * beside_all[3])
        )
        return weight * (values - jnp.take(value_sums / weight_sums, offset))

    stored_table = make_phase(longitude, order_map)

    def phases():
        return stored_table

    def node_part(vector, observed):
        nodal = jnp.einsum(
            "mkn,cmn->kcm", legendre.astype(jnp.float32), vector, precision=lax.Precision.HIGHEST
        ).reshape(node_count, 2 * slot_count)
        row_terms = lax.dot_general(
            selector, nodal, (((0,), (0,)), ((), ())), precision=lax.Precision.HIGHEST
        )
        partial_rows = jnp.sum(row_terms * phases(), axis=1)
        predicted = lax.psum(partial_rows, "order")
        centered = center_rows(observed - predicted)
        node_terms = jnp.dot(
            selector, phases() * centered[:, None], precision=lax.Precision.HIGHEST
        )
        return node_terms.reshape(node_count, 2, slot_count)

    def lifted(node_terms):
        return jnp.einsum(
            "mkn,kcm->cmn",
            legendre.astype(jnp.float32),
            node_terms,
            precision=lax.Precision.HIGHEST,
        )

    no_data = jnp.zeros_like(gradient)
    iterate = start_iterate * valid_mask
    new_direction = direction * valid_mask

    def summed(vector, observed):
        return lifted(lax.psum(node_part(vector, observed), "tm"))

    def pair_sum(first, second):
        return lax.psum((first, second), "order")

    def single_sum(value):
        return lax.psum(value, "order")

    residual = valid_mask * (summed(iterate, gradient) - kaula_prior * iterate)
    return run_steps(
        residual,
        iterate,
        new_direction,
        valid_mask,
        kaula_prior,
        precond,
        lambda vector: summed(vector, no_data),
        pair_sum,
        single_sum,
    )


def solution(mesh):
    placed = (
        P("tm"),
        P("tm"),
        P("tm"),
        P("tm"),
        P("tm"),
        P("order"),
        P("order", None, None),
        P(None, None, "order", None),
        P(None, "order", None),
        P(None, "order", None),
        P(None, "order", None),
    )
    return jax.shard_map(
        shards,
        mesh=mesh,
        in_specs=placed,
        out_specs=(P(None, "order", None), P(None, "order", None), P(None, "order", None)),
        check_vma=False,
    )
```

profile of v0, /device:TPU:0, one launch (start us, length us, event | category | flops | bytes accessed | tf_op | source)
XLA Modules:
  0.0 635.9 jit_solution(18027174269071761478)
XLA Ops:
  7.2 1.3 fusion.54
  8.5 1.4 fusion.32
  11.2 1.4 fusion.48
  12.5 29.0 %scatter_custom_fusion.1 = f32[4096]{0:T(1024)S(1)} fusion(s32[4096]{0:T(1024)S(1)} %get-tuple-element.117, f32[4096]{0:T(1024)} %param.31, f32[]{:T(128)} %constant.182.clone.1), kind=kCustom, calls=%fused_computation.86 | custom fusion | flops 4096 | bytes 16896 | tf_op jit(solution)/shard_map/scatter-add | solution.py:99
  42.1 1.4 maximum_bitcast_fusion
  43.6 1.3 collective-permute-start.2
  44.9 5.5 collective-permute-start
  52.0 12.4 %convolution_bitcast_fusion.4 = f32[160,2,76]{0,1,2:T(2,128)S(1)} fusion(bf16[76,160,304]{2,1,0:T(8,128)(2,1)} %param.35, f32[2,76,304]{2,0,1:T(2,128)} %param.39, pred[2,76]{0,1:T(8,128)(4,1)S(1)} %broadcast_or_fusion, pred[76,304]{1,0:T(8,128)(4,1)S(1)} %fusion.28), kind=kOutput, calls=%fused_computation.46 | convolution fusion | flops 88811776 | bytes 7698648 | tf_op jit(solution)/shard_map/mkn,cmn->kcm/dot_general | solution.py:132
  64.4 12.7 %convolution_bitcast_fusion.5 = f32[160,2,76]{0,1,2:T(2,128)S(1)} fusion(bf16[76,160,304]{2,1,0:T(8,128)(2,1)} %param.35, f32[2,76,304]{2,0,1:T(2,128)S(1)} %copy-done.5, pred[2,76]{0,1:T(8,128)(4,1)S(1)} %broadcast_or_fusion, pred[76,304]{1,0:T(8,128)(4,1)S(1)} %fusion.28), kind=kOutput, calls=%fused_computation.47 | convolution fusion | flops 88811776 | bytes 7698648 | tf_op jit(solution)/shard_map/mkn,cmn->kcm/dot_general | solution.py:132
  77.9 4.6 multiply_cosine_fusion
  82.5 1.5 fusion.11
  84.1 1.5 fusion.10
  85.6 11.0 %all-reduce.3 = (f32[4096]{0:T(1024)S(1)}, f32[4096]{0:T(1024)S(1)}) all-reduce(f32[4096]{0:T(1024)S(1)} %fusion.11, f32[4096]{0:T(1024)S(1)} %fusion.10), channel_id=1, replica_groups=mesh['tm'=8,'order'=4] {'order'}, use_global_device_ids=true, to_apply=%region_8.10 | all-reduce | flops 8192 | bytes 65536 | tf_op jit(solution)/shard_map/psum | solution.py:139
  96.6 28.8 %scatter_custom_fusion = f32[4096]{0:T(1024)S(1)} fusion(s32[4096]{0:T(1024)S(1)} %get-tuple-element.117, f32[4096]{0:T(1024)S(1)} %get-tuple-element.114, f32[]{:T(128)} %constant.182.clone.1), kind=kCustom, calls=%fused_computation.88 | custom fusion | flops 4096 | bytes 16388 | tf_op jit(solution)/shard_map/scatter-add | solution.py:115
  126.0 4.8 collective-permute-start.1
  130.9 28.8 %scatter_custom_fusion.2 = f32[4096]{0:T(1024)S(1)} fusion(s32[4096]{0:T(1024)S(1)} %get-tuple-element.117, f32[4096]{0:T(1024)S(1)} %get-tuple-element.128, f32[]{:T(128)} %constant.182.clone.1), kind=kCustom, calls=%fused_computation.84 | custom fusion | flops 4096 | bytes 16388 | tf_op jit(solution)/shard_map/scatter-add | solution.py:115
  160.3 2.6 collective-permute-start.4
  167.0 1.3 collective-permute-start.3
  169.4 1.3 collective-permute-start.5
  174.0 1.8 collective-permute-done.5
  176.8 23.2 %gather_fusion.1 = f32[4096]{0:T(1024)S(1)} fusion(f32[4096]{0:T(1024)S(1)} %get-tuple-element.124, s32[4096]{0:T(1024)S(1)} %get-tuple-element.116), kind=kCustom, calls=%fused_computation.1.clone | custom fusion | bytes 49152 | tf_op jit(solution)/shard_map/jit(_take)/gather | solution.py:124
  200.0 23.0 %gather_fusion = f32[4096]{0:T(1024)S(1)} fusion(f32[4096]{0:T(1024)S(1)} %get-tuple-element.125, s32[4096]{0:T(1024)S(1)} %get-tuple-element.116), kind=kCustom, calls=%fused_computation.clone | custom fusion | bytes 49152 | tf_op jit(solution)/shard_map/jit(_take)/gather | solution.py:124
  223.0 1.8 fusion.6
  225.7 1.8 fusion.5
  228.5 5.0 copy.22
  233.5 17.6 %reshape.343 = f32[19,2432,19]{2,1,0:T(8,128)} reshape(f32[19,2,76,304]{3,2,1,0:T(8,128)} %copy.22) | data formatting | bytes 7023616 | tf_op jit(solution)/shard_map/reshape | solution.py:44
  251.1 50.9 %all-reduce.9.cloned.1.call-done = (f32[160,2,76]{0,1,2:T(2,128)}, f32[160,2,76]{0,1,2:T(2,128)}) async-done(((f32[160,2,76]{0,1,2:T(2,128)}, f32[160,2,76]{0,1,2:T(2,128)}), (f32[160,2,76]{0,1,2:T(2,128)}, f32[160,2,76]{0,1,2:T(2,128)})) %all-reduce.9.cloned.1.call-update) | async-done | bytes 194576 | tf_op jit(solution)/shard_map/psum | solution.py:159
  302.1 8.2 %fusion.27 = f32[2,76,304]{2,0,1:T(2,128)S(1)} fusion(f32[160,2,76]{0,1,2:T(2,128)} %get-tuple-element.105, bf16[76,160,304]{2,1,0:T(8,128)(2,1)} %param.35, f32[2,76,304]{2,0,1:T(2,128)S(1)} %copy-done.11, pred[2,76]{0,1:T(8,128)(4,1)S(1)} %broadcast_or_fusion, pred[76,304]{1,0:T(8,128)(4,1)S(1)} %fusion.28, f32[2,76,304]{2,0,1:T(2,128)S(1)} %copy-done.5), kind=kOutput, calls=%fused_computation.44 | convolution fusion | flops 88950400 | bytes 8068312 | tf_op jit(solution)/shard_map/mkn,kcm->cmn/dot_general | solution.py:147
  310.3 8.1 %multiply_reduce_fusion.4 = (f32[]{:T(128)}, f32[]{:T(128)}, f32[2,76,304]{2,0,1:T(2,128)S(1)}) fusion(f32[2,76,304]{2,0,1:T(2,128)S(1)} %copy-done, pred[2,76]{0,1:T(8,128)(4,1)S(1)} %broadcast_or_fusion, pred[76,304]{1,0:T(8,128)(4,1)S(1)} %fusion.28, f32[2,76,304]{2,0,1:T(2,128)S(1)} %fusion.27, f32[160,2,76]{0,1,2:T(2,128)S(1)} %copy-done.13, ...), kind=kOutput, calls=%fused_computation.61 | convolution fusion | flops 89135232 | bytes 8253152 | tf_op jit(solution)/shard_map/mkn,kcm->cmn/dot_general | solution.py:147
  318.3 6.3 all-reduce.2
  326.8 49.5 %fusion.2 = f32[2432,1,19]{2,1,0:T(1,128)S(1)} fusion(f32[2432,19,1]{1,2,0:T(1,128)S(1)} %bitcast.90, f32[19,2432,19]{2,1,0:T(8,128)} %reshape.343), kind=kOutput, calls=%fused_computation.9 | convolution fusion | flops 10535424 | bytes 3881472 | tf_op jit(solution)/shard_map/jbi,bj->bi/dot_general | solution.py:45
  377.9 7.2 %psum.90 = f32[]{:T(128)} all-reduce(f32[]{:T(128)} %multiply_reduce_fusion.3), channel_id=1, replica_groups=mesh['tm'=8,'order'=4] {'order'}, use_global_device_ids=true, to_apply=%region_14.16 | all-reduce | flops 1 | bytes 8 | tf_op jit(solution)/shard_map/psum | solution.py:165
  386.7 12.2 %convolution_bitcast_fusion.3 = f32[160,2,76]{0,1,2:T(2,128)S(1)} fusion(f32[2,76,304]{2,0,1:T(2,128)S(1)} %multiply_subtract_fusion.2, bf16[76,160,304]{2,1,0:T(8,128)(2,1)} %param.35), kind=kOutput, calls=%fused_computation.45 | convolution fusion | flops 88719360 | bytes 7675392 | tf_op jit(solution)/shard_map/mkn,cmn->kcm/dot_general | solution.py:132
  399.0 2.8 fusion.12
  401.9 10.2 %psum.92 = f32[4096]{0:T(1024)S(1)} all-reduce(f32[4096]{0:T(1024)S(1)} %fusion.12), channel_id=1, replica_groups=mesh['tm'=8,'order'=4] {'order'}, use_global_device_ids=true, to_apply=%region_18.20 | all-reduce | flops 4096 | bytes 32768 | tf_op jit(solution)/shard_map/psum | solution.py:139
  412.1 28.8 %scatter_custom_fusion.3 = f32[4096]{0:T(1024)S(1)} fusion(s32[4096]{0:T(1024)S(1)} %get-tuple-element.117, f32[4096]{0:T(1024)S(1)} %subtract_multiply_fusion, f32[]{:T(128)} %constant.182.clone.1), kind=kCustom, calls=%fused_computation.82 | custom fusion | flops 4096 | bytes 16388 | tf_op jit(solution)/shard_map/scatter-add | solution.py:115
  441.5 3.1 collective-permute-start.6
  446.7 1.3 collective-permute-start.7
  448.0 4.5 collective-permute-done.7
  453.4 23.0 %gather_fusion.2 = f32[4096]{0:T(1024)S(1)} fusion(f32[4096]{0:T(1024)S(1)} %fusion.33, s32[4096]{0:T(1024)S(1)} %get-tuple-element.116), kind=kCustom, calls=%fused_computation.2.clone | custom fusion | bytes 49152 | tf_op jit(solution)/shard_map/jit(_take)/gather | solution.py:124
  476.4 3.2 fusion.4
  480.5 70.8 %all-reduce.7.cloned.1.call-done = f32[160,2,76]{0,1,2:T(2,128)} async-done(((f32[160,2,76]{0,1,2:T(2,128)}), f32[160,2,76]{0,1,2:T(2,128)}) %all-reduce.7.cloned.1.call-update) | async-done | bytes 97296 | tf_op jit(solution)/shard_map/psum | solution.py:159
  551.3 8.8 %multiply_reduce_fusion.1 = (f32[]{:T(128)}, f32[]{:T(128)}, f32[2,76,304]{2,0,1:T(2,128)S(1)}) fusion(f32[2,76,304]{2,0,1:T(2,128)S(1)} %multiply_subtract_fusion.2, f32[2,76,304]{2,0,1:T(2,128)S(1)} %bitcast.93, f32[160,2,76]{0,1,2:T(2,128)} %all-reduce.7.cloned.1.call-done, bf16[76,160,304]{2,1,0:T(8,128)(2,1)} %param.35, ...), kind=kOutput, calls=%fused_computation.56 | convolution fusion | flops 89089024 | bytes 8253152 | tf_op jit(solution)/shard_map/mkn,kcm->cmn/dot_general | solution.py:147
  560.0 6.3 all-reduce.1
  568.5 48.9 %fusion = f32[2432,1,19]{2,1,0:T(1,128)S(1)} fusion(f32[2432,19,1]{1,2,0:T(1,128)S(1)} %bitcast.88, f32[19,2432,19]{2,1,0:T(8,128)} %reshape.343), kind=kOutput, calls=%fused_computation.7 | convolution fusion | flops 10535424 | bytes 3881472 | tf_op jit(solution)/shard_map/jbi,bj->bi/dot_general | solution.py:45
  618.1 1.0 multiply_reduce_fusion
  619.1 7.2 %psum.95 = f32[]{:T(128)} all-reduce(f32[]{:T(128)} %multiply_reduce_fusion), channel_id=1, replica_groups=mesh['tm'=8,'order'=4] {'order'}, use_global_device_ids=true, to_apply=%region_24.26 | all-reduce | flops 1 | bytes 8 | tf_op jit(solution)/shard_map/psum | solution.py:165
  627.7 1.2 multiply_subtract_fusion
  (92 shorter events, 16.4 us)
Async XLA Ops:
  7.2 294.9 %all-reduce.9.cloned.1.call-start = ((), (), s32[]{:S(2)}) async-start(), calls=%async_computation.1 | async-start | bytes 622592 | tf_op jit(solution)/shard_map/psum | solution.py:159
  43.6 127.2 %collective-permute-start.2 = (f32[2,1]{1,0:T(2,128)S(1)}, f32[2,1]{1,0:T(2,128)S(1)}, u32[]{:S(2)}, u32[]{:S(2)}) collective-permute-start(f32[2,1]{1,0:T(2,128)S(1)} %get-tuple-element.139), channel_id=1, source_target_pairs={{4,0},{8,4},{12,8},{16,12},{20,16},{24,20},{28,24},{5,1},{9,5},{13... | collective-permute-start | bytes 32 | tf_op jit(solution)/shard_map/ppermute | solution.py:19
  44.9 118.6 %collective-permute-start = (f32[2,1]{1,0:T(2,128)S(1)}, f32[2,1]{1,0:T(2,128)S(1)}, u32[]{:S(2)}, u32[]{:S(2)}) collective-permute-start(f32[2,1]{1,0:T(2,128)S(1)} %get-tuple-element.140), channel_id=1, source_target_pairs={{0,4},{4,8},{8,12},{12,16},{16,20},{20,24},{24,28},{1,5},{5,9},{9,... | collective-permute-start | bytes 32 | tf_op jit(solution)/shard_map/ppermute | solution.py:18
  52.0 12.4 %copy-start.5 = (f32[2,76,304]{2,0,1:T(2,128)S(1)}, f32[2,76,304]{2,0,1:T(2,128)}, u32[]{:S(2)}) copy-start(f32[2,76,304]{2,0,1:T(2,128)} %param.38) | copy-start | bytes 554500
  64.4 13.5 %copy-start.9 = (f32[4096]{0:T(1024)S(1)}, f32[4096]{0:T(1024)}, u32[]{:S(2)}) copy-start(f32[4096]{0:T(1024)} %param.29) | copy-start | bytes 49156
  77.2 5.3 copy-start.14
  82.5 143.2 %copy-start.1 = (f32[4096,76]{0,1:T(8,128)}, f32[4096,76]{0,1:T(8,128)S(1)}, u32[]{:S(2)}) copy-start(f32[4096,76]{0,1:T(8,128)S(1)} %get-tuple-element.120) | copy-start | bytes 3735556
  82.5 143.2 %copy-start.3 = (f32[4096,76]{0,1:T(8,128)}, f32[4096,76]{0,1:T(8,128)S(1)}, u32[]{:S(2)}) copy-start(f32[4096,76]{0,1:T(8,128)S(1)} %get-tuple-element.121) | copy-start | bytes 3735556
  82.5 1.5 copy-start.8
  84.0 12.6 %copy-start.7 = (f32[4096]{0:T(1024)S(1)}, f32[4096]{0:T(1024)}, u32[]{:S(2)}) copy-start(f32[4096]{0:T(1024)} %param.31) | copy-start | bytes 49156
  84.0 12.6 %copy-start.10 = (f32[4096]{0:T(1024)S(1)}, f32[4096]{0:T(1024)}, u32[]{:S(2)}) copy-start(f32[4096]{0:T(1024)} %param.32) | copy-start | bytes 49156
  126.0 39.9 %collective-permute-start.1 = (f32[1]{0:T(128)}, f32[1]{0:T(128)}, u32[]{:S(2)}, u32[]{:S(2)}) collective-permute-start(f32[1]{0:T(128)} %dynamic_slice.13), channel_id=1, source_target_pairs={{0,4},{4,8},{8,12},{12,16},{16,20},{20,24},{24,28},{1,5},{5,9},{9,... | collective-permute-start | bytes 20 | tf_op jit(solution)/shard_map/ppermute | solution.py:18
  160.3 8.0 %collective-permute-start.4 = (f32[1]{0:T(128)}, f32[1]{0:T(128)}, u32[]{:S(2)}, u32[]{:S(2)}) collective-permute-start(f32[1]{0:T(128)} %dynamic_slice.14), channel_id=1, source_target_pairs={{0,4},{4,8},{8,12},{12,16},{16,20},{20,24},{24,28},{1,5},{5,9},{9,... | collective-permute-start | bytes 20 | tf_op jit(solution)/shard_map/ppermute | solution.py:18
  167.0 6.4 %collective-permute-start.3 = (f32[1]{0:T(128)}, f32[1]{0:T(128)}, u32[]{:S(2)}, u32[]{:S(2)}) collective-permute-start(f32[1]{0:T(128)} %get-tuple-element.129), channel_id=1, source_target_pairs={{4,0},{8,4},{12,8},{16,12},{20,16},{24,20},{28,24},{5,1},{9,5},{13... | collective-permute-start | bytes 20 | tf_op jit(solution)/shard_map/ppermute | solution.py:19
  169.4 6.3 collective-permute-start.5
  228.4 322.9 %all-reduce.7.cloned.1.call-start = ((), (), s32[]{:S(2)}) async-start(), calls=%async_computation | async-start | bytes 311296 | tf_op jit(solution)/shard_map/psum | solution.py:159
  233.5 68.6 %copy-start.11 = (f32[2,76,304]{2,0,1:T(2,128)S(1)}, f32[2,76,304]{2,0,1:T(2,128)}, u32[]{:S(2)}) copy-start(f32[2,76,304]{2,0,1:T(2,128)} %param.37) | copy-start | bytes 554500
  302.1 8.2 %copy-start = (f32[2,76,304]{2,0,1:T(2,128)S(1)}, f32[2,76,304]{2,0,1:T(2,128)}, u32[]{:S(2)}) copy-start(f32[2,76,304]{2,0,1:T(2,128)} %param.39) | copy-start | bytes 554500
  302.1 8.2 %copy-start.13 = (f32[160,2,76]{0,1,2:T(2,128)S(1)}, f32[160,2,76]{0,1,2:T(2,128)}, u32[]{:S(2)}) copy-start(f32[160,2,76]{0,1,2:T(2,128)} %get-tuple-element.104) | copy-start | bytes 291844
  386.7 12.3 %copy-start.2 = (f32[4096,76]{0,1:T(8,128)S(1)}, f32[4096,76]{0,1:T(8,128)}, u32[]{:S(2)}) copy-start(f32[4096,76]{0,1:T(8,128)} %copy-done.1) | copy-start | bytes 3735556
  441.5 4.0 collective-permute-start.6
  446.7 5.8 collective-permute-start.7
  476.4 74.9 %copy-start.12 = (f32[2,76,304]{2,0,1:T(2,128)S(1)}, f32[2,76,304]{2,0,1:T(2,128)}, u32[]{:S(2)}) copy-start(f32[2,76,304]{2,0,1:T(2,128)} %param.37) | copy-start | bytes 554500
  567.7 0.8 copy-start.4
  568.5 59.1 %copy-start.6 = (f32[2,76,304]{2,0,1:T(2,128)S(1)}, f32[2,76,304]{2,0,1:T(2,128)}, u32[]{:S(2)}) copy-start(f32[2,76,304]{2,0,1:T(2,128)} %param.38) | copy-start | bytes 554500
Sparse Core Ops, SparseCore 0:
  228.5 73.4 all-reduce.8
  480.6 70.6 all-reduce.6
where the time goes:
time: 643 us; the launch traced here: 636 us
  matrix products  173 us (27%)
  other arithmetic  132 us (21%)
  waiting for transfers between devices  129 us (20%)
  local copies, waits for them, and re-layouts  103 us (16%)
  blocking collectives  48.2 us (7%)
  between operations  29.1 us (5%)
  starting transfers between devices  21.3 us (3%)
    psum x2, waiting for transfers between devices, summed(): return lifted(lax.psum(node_part(vector, observed), 'tm'))  122 us
    dot_general x2, matrix products, precondition(): jnp.einsum('jbi,bj->bi', shaped, flat.reshape(block_count, DB), precision...  98.4 us
    scatter-add x3, other arithmetic, center_rows(): jax.ops.segment_sum(weight * values, offset, num_segments=row_count)  86.4 us
    gather x3, local copies, waits for them, and re-layouts, center_rows(): return weight * (values - jnp.take(value_sums / weight_sums, offset))  69.3 us
    dot_general x3, matrix products, node_part(): jnp.einsum('mkn,cmn->kcm', legendre.astype(jnp.float32), vector, precisio...  37.3 us
    scatter-add x1, other arithmetic, shards(): weight_sums = jax.ops.segment_sum(weight, offset, num_segments=row_count)  29 us
    dot_general x3, matrix products, lifted(): jnp.einsum('mkn,kcm->cmn', legendre.astype(jnp.float32), node_terms, prec...  25 us
    psum x2, blocking collectives, node_part(): predicted = lax.psum(partial_rows, 'order')  21.3 us
  transfers between devices with their start and end apart: 10, of which 5 were waited for; matrix products, arithmetic and copies ran while one was open for 19% of the time, Pallas kernels for 0%

commit v1 on v0

--- a/solution.py
+++ b/solution.py
@@ -156,7 +156,7 @@
     new_direction = direction * valid_mask
 
     def summed(vector, observed):
-        return lifted(lax.psum(node_part(vector, observed), "tm"))
+        return lifted(jnp.sum(lax.all_gather(node_part(vector, observed), "tm"), axis=0))
 
     def pair_sum(first, second):
         return lax.psum((first, second), "order")

time: 643 us -> 611 us (0.950)
  waiting for transfers between devices: 129 us -> 7.2 us
  blocking collectives: 48.2 us -> 152 us
  between operations: 29.1 us -> 15.7 us
    psum x2 -> x0, waiting for transfers between devices: 122 us -> none  [summed(): return lifted(lax.psum(node_part(vector, observed), 'tm'))]
    all_gather x0 -> x3, blocking collectives: none -> 104 us  [summed(): lax.all_gather(node_part(vector, observed), 'tm')]
  transfers between devices with their start and end apart: 10 -> 8, of which waited for: 5 -> 3; matrix products, arithmetic and copies ran while one was open for 19% -> 20% of each run, Pallas kernels for 0% -> 0%
where the time goes in v1:
time: 611 us; the launch traced here: 604 us
  matrix products  173 us (28%)
  blocking collectives  152 us (25%)
  other arithmetic  134 us (22%)
  local copies, waits for them, and re-layouts  102 us (17%)
  starting transfers between devices  20.8 us (3%)
  between operations  15.7 us (3%)
  waiting for transfers between devices  7.2 us (1%)
    all_gather x3, blocking collectives, summed(): lax.all_gather(node_part(vector, observed), 'tm')  104 us
    dot_general x2, matrix products, precondition(): jnp.einsum('jbi,bj->bi', shaped, flat.reshape(block_count, DB), precision...  98.3 us
    scatter-add x3, other arithmetic, center_rows(): jax.ops.segment_sum(weight * values, offset, num_segments=row_count)  86.4 us
    gather x3, local copies, waits for them, and re-layouts, center_rows(): return weight * (values - jnp.take(value_sums / weight_sums, offset))  69.1 us
    dot_general x3, matrix products, node_part(): jnp.einsum('mkn,cmn->kcm', legendre.astype(jnp.float32), vector, precisio...  37.3 us
    scatter-add x1, other arithmetic, shards(): weight_sums = jax.ops.segment_sum(weight, offset, num_segments=row_count)  29 us
    dot_general x3, matrix products, lifted(): jnp.einsum('mkn,kcm->cmn', legendre.astype(jnp.float32), node_terms, prec...  23.6 us
    psum x2, blocking collectives, node_part(): predicted = lax.psum(partial_rows, 'order')  21.3 us
  transfers between devices with their start and end apart: 8, of which 3 were waited for; matrix products, arithmetic and copies ran while one was open for 20% of the time, Pallas kernels for 0%

profile of v1, /device:TPU:0, one launch (start us, length us, event | category | flops | bytes accessed | tf_op | source)
XLA Modules:
  0.0 603.9 jit_solution(2805876738427737516)
XLA Ops:
  0.6 1.3 fusion.54
  1.9 1.4 fusion.32
  4.6 1.4 fusion.48
  6.0 29.0 %scatter_custom_fusion.1 = f32[4096]{0:T(1024)S(1)} fusion(s32[4096]{0:T(1024)S(1)} %get-tuple-element.115, f32[4096]{0:T(1024)} %param.31, f32[]{:T(128)} %constant.182.clone.1), kind=kCustom, calls=%fused_computation.86 | custom fusion | flops 4096 | bytes 16896 | tf_op jit(solution)/shard_map/scatter-add | solution.py:99
  35.5 1.4 maximum_bitcast_fusion
  37.0 1.3 collective-permute-start.2
  38.3 5.5 collective-permute-start
  45.4 12.4 %convolution_bitcast_fusion.4 = f32[160,2,76]{0,1,2:T(2,128)S(1)} fusion(bf16[76,160,304]{2,1,0:T(8,128)(2,1)} %param.35, f32[2,76,304]{2,0,1:T(2,128)} %param.39, pred[2,76]{0,1:T(8,128)(4,1)S(1)} %broadcast_or_fusion, pred[76,304]{1,0:T(8,128)(4,1)S(1)} %fusion.28), kind=kOutput, calls=%fused_computation.46 | convolution fusion | flops 88811776 | bytes 7698648 | tf_op jit(solution)/shard_map/mkn,cmn->kcm/dot_general | solution.py:132
  57.9 12.7 %convolution_bitcast_fusion.5 = f32[160,2,76]{0,1,2:T(2,128)S(1)} fusion(bf16[76,160,304]{2,1,0:T(8,128)(2,1)} %param.35, f32[2,76,304]{2,0,1:T(2,128)S(1)} %copy-done.5, pred[2,76]{0,1:T(8,128)(4,1)S(1)} %broadcast_or_fusion, pred[76,304]{1,0:T(8,128)(4,1)S(1)} %fusion.28), kind=kOutput, calls=%fused_computation.47 | convolution fusion | flops 88811776 | bytes 7698648 | tf_op jit(solution)/shard_map/mkn,cmn->kcm/dot_general | solution.py:132
  71.3 4.6 multiply_cosine_fusion
  75.9 1.5 fusion.11
  77.5 1.5 fusion.10
  79.0 11.0 %all-reduce.2 = (f32[4096]{0:T(1024)S(1)}, f32[4096]{0:T(1024)S(1)}) all-reduce(f32[4096]{0:T(1024)S(1)} %fusion.11, f32[4096]{0:T(1024)S(1)} %fusion.10), channel_id=1, replica_groups=mesh['tm'=8,'order'=4] {'order'}, use_global_device_ids=true, to_apply=%region_8.10 | all-reduce | flops 8192 | bytes 65536 | tf_op jit(solution)/shard_map/psum | solution.py:139
  90.1 28.8 %scatter_custom_fusion = f32[4096]{0:T(1024)S(1)} fusion(s32[4096]{0:T(1024)S(1)} %get-tuple-element.115, f32[4096]{0:T(1024)S(1)} %get-tuple-element.112, f32[]{:T(128)} %constant.182.clone.1), kind=kCustom, calls=%fused_computation.88 | custom fusion | flops 4096 | bytes 16388 | tf_op jit(solution)/shard_map/scatter-add | solution.py:115
  119.5 4.8 collective-permute-start.1
  124.3 28.8 %scatter_custom_fusion.2 = f32[4096]{0:T(1024)S(1)} fusion(s32[4096]{0:T(1024)S(1)} %get-tuple-element.115, f32[4096]{0:T(1024)S(1)} %get-tuple-element.126, f32[]{:T(128)} %constant.182.clone.1), kind=kCustom, calls=%fused_computation.84 | custom fusion | flops 4096 | bytes 16388 | tf_op jit(solution)/shard_map/scatter-add | solution.py:115
  153.7 2.6 collective-permute-start.4
  156.9 5.0 copy.31
  161.9 17.7 %reshape.332 = f32[19,2432,19]{2,1,0:T(8,128)} reshape(f32[19,2,76,304]{3,2,1,0:T(8,128)} %copy.31) | data formatting | bytes 7023616 | tf_op jit(solution)/shard_map/reshape | solution.py:44
  183.2 1.3 collective-permute-start.3
  185.7 1.3 collective-permute-start.5
  190.3 1.7 collective-permute-done.5
  193.0 23.0 %gather_fusion.1 = f32[4096]{0:T(1024)S(1)} fusion(f32[4096]{0:T(1024)S(1)} %get-tuple-element.122, s32[4096]{0:T(1024)S(1)} %get-tuple-element.114), kind=kCustom, calls=%fused_computation.1.clone | custom fusion | bytes 49152 | tf_op jit(solution)/shard_map/jit(_take)/gather | solution.py:124
  216.0 23.0 %gather_fusion = f32[4096]{0:T(1024)S(1)} fusion(f32[4096]{0:T(1024)S(1)} %get-tuple-element.123, s32[4096]{0:T(1024)S(1)} %get-tuple-element.114), kind=kCustom, calls=%fused_computation.clone | custom fusion | bytes 49152 | tf_op jit(solution)/shard_map/jit(_take)/gather | solution.py:124
  239.1 1.8 fusion.6
  241.1 2.5 fusion.5
  244.7 36.6 %all_gather.10 = f32[8,160,2,76]{1,2,3,0:T(2,128)S(1)} all-gather(f32[1,160,2,76]{1,2,3,0:T(2,128)S(1)} %copy.27), channel_id=1, replica_groups=mesh['tm'=8,'order'=4] {'tm'}, dimensions={0}, use_global_device_ids=true | all-gather | bytes 875520 | tf_op jit(solution)/shard_map/all_gather | solution.py:159
  282.0 33.2 %all_gather.9 = f32[8,160,2,76]{1,2,3,0:T(2,128)S(1)} all-gather(f32[1,160,2,76]{1,2,3,0:T(2,128)S(1)} %copy.23), channel_id=1, replica_groups=mesh['tm'=8,'order'=4] {'tm'}, dimensions={0}, use_global_device_ids=true | all-gather | bytes 875520 | tf_op jit(solution)/shard_map/all_gather | solution.py:159
  315.9 7.5 %fusion.27 = f32[2,76,304]{2,0,1:T(2,128)S(1)} fusion(f32[160,2,76]{0,1,2:T(2,128)S(1)} %reduce_sum.109, bf16[76,160,304]{2,1,0:T(8,128)(2,1)} %param.35, f32[2,76,304]{2,0,1:T(2,128)S(1)} %copy-done.11, pred[2,76]{0,1:T(8,128)(4,1)S(1)} %broadcast_or_fusion, pred[76,304]{1,0:T(8,128)(4,1)S(1)} %fusion.28, f32[2,76,304]{2,0,1:T(2,128)S(1)} %copy-done.5), kind=kOutput, calls=%fused_computation.44 | convolution fusion | flops 88950400 | bytes 8068312 | tf_op jit(solution)/shard_map/mkn,kcm->cmn/dot_general | solution.py:147
  323.4 8.1 %multiply_reduce_fusion.4 = (f32[]{:T(128)}, f32[]{:T(128)}, f32[2,76,304]{2,0,1:T(2,128)S(1)}) fusion(f32[2,76,304]{2,0,1:T(2,128)S(1)} %copy-done, pred[2,76]{0,1:T(8,128)(4,1)S(1)} %broadcast_or_fusion, pred[76,304]{1,0:T(8,128)(4,1)S(1)} %fusion.28, f32[2,76,304]{2,0,1:T(2,128)S(1)} %fusion.27, f32[160,2,76]{0,1,2:T(2,128)S(1)} %reduce_sum.112, ...), kind=kOutput, calls=%fused_computation.61 | convolution fusion | flops 89135232 | bytes 8253152 | tf_op jit(solution)/shard_map/mkn,kcm->cmn/dot_general | solution.py:147
  331.4 6.3 %all-reduce.1 = (f32[]{:T(128)}, f32[]{:T(128)}) all-reduce(f32[]{:T(128)} %get-tuple-element.101, f32[]{:T(128)} %get-tuple-element.100), channel_id=1, replica_groups=mesh['tm'=8,'order'=4] {'order'}, use_global_device_ids=true, to_apply=%region_6.0 | all-reduce | flops 2 | bytes 16 | tf_op jit(solution)/shard_map/psum | solution.py:162
  339.9 49.4 %fusion.2 = f32[2432,1,19]{2,1,0:T(1,128)S(1)} fusion(f32[2432,19,1]{1,2,0:T(1,128)S(1)} %bitcast.90, f32[19,2432,19]{2,1,0:T(8,128)} %reshape.332), kind=kOutput, calls=%fused_computation.9 | convolution fusion | flops 10535424 | bytes 3881472 | tf_op jit(solution)/shard_map/jbi,bj->bi/dot_general | solution.py:45
  390.8 7.1 %psum.67 = f32[]{:T(128)} all-reduce(f32[]{:T(128)} %multiply_reduce_fusion.3), channel_id=1, replica_groups=mesh['tm'=8,'order'=4] {'order'}, use_global_device_ids=true, to_apply=%region_14.16 | all-reduce | flops 1 | bytes 8 | tf_op jit(solution)/shard_map/psum | solution.py:165
  399.6 12.2 %convolution_bitcast_fusion.3 = f32[160,2,76]{0,1,2:T(2,128)S(1)} fusion(f32[2,76,304]{2,0,1:T(2,128)S(1)} %multiply_subtract_fusion.2, bf16[76,160,304]{2,1,0:T(8,128)(2,1)} %param.35), kind=kOutput, calls=%fused_computation.45 | convolution fusion | flops 88719360 | bytes 7675392 | tf_op jit(solution)/shard_map/mkn,cmn->kcm/dot_general | solution.py:132
  412.0 2.8 fusion.12
  414.8 10.3 %psum.69 = f32[4096]{0:T(1024)S(1)} all-reduce(f32[4096]{0:T(1024)S(1)} %fusion.12), channel_id=1, replica_groups=mesh['tm'=8,'order'=4] {'order'}, use_global_device_ids=true, to_apply=%region_18.20 | all-reduce | flops 4096 | bytes 32768 | tf_op jit(solution)/shard_map/psum | solution.py:139
  425.1 28.8 %scatter_custom_fusion.3 = f32[4096]{0:T(1024)S(1)} fusion(s32[4096]{0:T(1024)S(1)} %get-tuple-element.115, f32[4096]{0:T(1024)S(1)} %subtract_multiply_fusion, f32[]{:T(128)} %constant.182.clone.1), kind=kCustom, calls=%fused_computation.82 | custom fusion | flops 4096 | bytes 16388 | tf_op jit(solution)/shard_map/scatter-add | solution.py:115
  454.5 2.7 collective-permute-start.6
  459.2 1.3 collective-permute-start.7
  460.5 4.6 collective-permute-done.7
  465.9 23.0 %gather_fusion.2 = f32[4096]{0:T(1024)S(1)} fusion(f32[4096]{0:T(1024)S(1)} %fusion.33, s32[4096]{0:T(1024)S(1)} %get-tuple-element.114), kind=kCustom, calls=%fused_computation.2.clone | custom fusion | bytes 49152 | tf_op jit(solution)/shard_map/jit(_take)/gather | solution.py:124
  489.0 3.2 fusion.4
  492.3 33.8 %all_gather.11 = f32[8,160,2,76]{1,2,3,0:T(2,128)S(1)} all-gather(f32[1,160,2,76]{1,2,3,0:T(2,128)S(1)} %copy.34), channel_id=1, replica_groups=mesh['tm'=8,'order'=4] {'tm'}, dimensions={0}, use_global_device_ids=true | all-gather | bytes 875520 | tf_op jit(solution)/shard_map/all_gather | solution.py:159
  526.8 8.1 %multiply_reduce_fusion.1 = (f32[]{:T(128)}, f32[]{:T(128)}, f32[2,76,304]{2,0,1:T(2,128)S(1)}) fusion(f32[2,76,304]{2,0,1:T(2,128)S(1)} %multiply_subtract_fusion.2, f32[2,76,304]{2,0,1:T(2,128)S(1)} %bitcast.93, f32[160,2,76]{0,1,2:T(2,128)S(1)} %reduce_sum.117, bf16[76,160,304]{2,1,0:T(8,128)(2,1)} %param.35, f32[2,76,304]{2,0,1:T(2,128)S(1)} %copy-done.12, ...), kind=kOutput, calls=%fused_computation.56 | convolution fusion | flops 89089024 | bytes 8253152 | tf_op jit(solution)/shard_map/mkn,kcm->cmn/dot_general | solution.py:147
  534.8 6.3 %all-reduce = (f32[]{:T(128)}, f32[]{:T(128)}) all-reduce(f32[]{:T(128)} %get-tuple-element.103, f32[]{:T(128)} %get-tuple-element.102), channel_id=1, replica_groups=mesh['tm'=8,'order'=4] {'order'}, use_global_device_ids=true, to_apply=%region_16.18 | all-reduce | flops 2 | bytes 16 | tf_op jit(solution)/shard_map/psum | solution.py:162
  543.3 49.0 %fusion = f32[2432,1,19]{2,1,0:T(1,128)S(1)} fusion(f32[2432,19,1]{1,2,0:T(1,128)S(1)} %bitcast.88, f32[19,2432,19]{2,1,0:T(8,128)} %reshape.332), kind=kOutput, calls=%fused_computation.7 | convolution fusion | flops 10535424 | bytes 3881472 | tf_op jit(solution)/shard_map/jbi,bj->bi/dot_general | solution.py:45
  593.9 7.1 %psum.71 = f32[]{:T(128)} all-reduce(f32[]{:T(128)} %multiply_reduce_fusion), channel_id=1, replica_groups=mesh['tm'=8,'order'=4] {'order'}, use_global_device_ids=true, to_apply=%region_24.26 | all-reduce | flops 1 | bytes 8 | tf_op jit(solution)/shard_map/psum | solution.py:165
  602.4 1.2 multiply_subtract_fusion
  (90 shorter events, 18.2 us)
Async XLA Ops:
  37.0 150.0 %collective-permute-start.2 = (f32[2,1]{1,0:T(2,128)S(1)}, f32[2,1]{1,0:T(2,128)S(1)}, u32[]{:S(2)}, u32[]{:S(2)}) collective-permute-start(f32[2,1]{1,0:T(2,128)S(1)} %get-tuple-element.137), channel_id=1, source_target_pairs={{4,0},{8,4},{12,8},{16,12},{20,16},{24,20},{28,24},{5,1},{9,5},{13... | collective-permute-start | bytes 32 | tf_op jit(solution)/shard_map/ppermute | solution.py:19
  38.3 141.3 %collective-permute-start = (f32[2,1]{1,0:T(2,128)S(1)}, f32[2,1]{1,0:T(2,128)S(1)}, u32[]{:S(2)}, u32[]{:S(2)}) collective-permute-start(f32[2,1]{1,0:T(2,128)S(1)} %get-tuple-element.138), channel_id=1, source_target_pairs={{0,4},{4,8},{8,12},{12,16},{16,20},{20,24},{24,28},{1,5},{5,9},{9,... | collective-permute-start | bytes 32 | tf_op jit(solution)/shard_map/ppermute | solution.py:18
  45.4 12.4 %copy-start.5 = (f32[2,76,304]{2,0,1:T(2,128)S(1)}, f32[2,76,304]{2,0,1:T(2,128)}, u32[]{:S(2)}) copy-start(f32[2,76,304]{2,0,1:T(2,128)} %param.38) | copy-start | bytes 554500
  57.9 13.5 %copy-start.9 = (f32[4096]{0:T(1024)S(1)}, f32[4096]{0:T(1024)}, u32[]{:S(2)}) copy-start(f32[4096]{0:T(1024)} %param.29) | copy-start | bytes 49156
  70.6 5.3 copy-start.13
  75.9 165.2 %copy-start.1 = (f32[4096,76]{0,1:T(8,128)}, f32[4096,76]{0,1:T(8,128)S(1)}, u32[]{:S(2)}) copy-start(f32[4096,76]{0,1:T(8,128)S(1)} %get-tuple-element.118) | copy-start | bytes 3735556
  75.9 165.2 %copy-start.3 = (f32[4096,76]{0,1:T(8,128)}, f32[4096,76]{0,1:T(8,128)S(1)}, u32[]{:S(2)}) copy-start(f32[4096,76]{0,1:T(8,128)S(1)} %get-tuple-element.119) | copy-start | bytes 3735556
  75.9 1.5 copy-start.8
  77.5 12.6 %copy-start.7 = (f32[4096]{0:T(1024)S(1)}, f32[4096]{0:T(1024)}, u32[]{:S(2)}) copy-start(f32[4096]{0:T(1024)} %param.31) | copy-start | bytes 49156
  77.5 12.6 %copy-start.10 = (f32[4096]{0:T(1024)S(1)}, f32[4096]{0:T(1024)}, u32[]{:S(2)}) copy-start(f32[4096]{0:T(1024)} %param.32) | copy-start | bytes 49156
  119.5 62.6 %collective-permute-start.1 = (f32[1]{0:T(128)}, f32[1]{0:T(128)}, u32[]{:S(2)}, u32[]{:S(2)}) collective-permute-start(f32[1]{0:T(128)} %dynamic_slice.13), channel_id=1, source_target_pairs={{0,4},{4,8},{8,12},{12,16},{16,20},{20,24},{24,28},{1,5},{5,9},{9,... | collective-permute-start | bytes 20 | tf_op jit(solution)/shard_map/ppermute | solution.py:18
  153.7 30.8 %collective-permute-start.4 = (f32[1]{0:T(128)}, f32[1]{0:T(128)}, u32[]{:S(2)}, u32[]{:S(2)}) collective-permute-start(f32[1]{0:T(128)} %dynamic_slice.14), channel_id=1, source_target_pairs={{0,4},{4,8},{8,12},{12,16},{16,20},{20,24},{24,28},{1,5},{5,9},{9,... | collective-permute-start | bytes 20 | tf_op jit(solution)/shard_map/ppermute | solution.py:18
  183.2 6.4 %collective-permute-start.3 = (f32[1]{0:T(128)}, f32[1]{0:T(128)}, u32[]{:S(2)}, u32[]{:S(2)}) collective-permute-start(f32[1]{0:T(128)} %get-tuple-element.127), channel_id=1, source_target_pairs={{4,0},{8,4},{12,8},{16,12},{20,16},{24,20},{28,24},{5,1},{9,5},{13... | collective-permute-start | bytes 20 | tf_op jit(solution)/shard_map/ppermute | solution.py:19
  185.7 6.3 %collective-permute-start.5 = (f32[1]{0:T(128)}, f32[1]{0:T(128)}, u32[]{:S(2)}, u32[]{:S(2)}) collective-permute-start(f32[1]{0:T(128)} %get-tuple-element.124), channel_id=1, source_target_pairs={{4,0},{8,4},{12,8},{16,12},{20,16},{24,20},{28,24},{5,1},{9,5},{13... | collective-permute-start | bytes 20 | tf_op jit(solution)/shard_map/ppermute | solution.py:19
  244.7 71.1 %copy-start.11 = (f32[2,76,304]{2,0,1:T(2,128)S(1)}, f32[2,76,304]{2,0,1:T(2,128)}, u32[]{:S(2)}) copy-start(f32[2,76,304]{2,0,1:T(2,128)} %param.37) | copy-start | bytes 554500
  315.8 7.5 %copy-start = (f32[2,76,304]{2,0,1:T(2,128)S(1)}, f32[2,76,304]{2,0,1:T(2,128)}, u32[]{:S(2)}) copy-start(f32[2,76,304]{2,0,1:T(2,128)} %param.39) | copy-start | bytes 554500
  399.6 12.3 %copy-start.2 = (f32[4096,76]{0,1:T(8,128)S(1)}, f32[4096,76]{0,1:T(8,128)}, u32[]{:S(2)}) copy-start(f32[4096,76]{0,1:T(8,128)} %copy-done.1) | copy-start | bytes 3735556
  454.5 3.5 collective-permute-start.6
  459.2 5.9 collective-permute-start.7
  492.1 34.6 %copy-start.12 = (f32[2,76,304]{2,0,1:T(2,128)S(1)}, f32[2,76,304]{2,0,1:T(2,128)}, u32[]{:S(2)}) copy-start(f32[2,76,304]{2,0,1:T(2,128)} %param.37) | copy-start | bytes 554500
  542.5 0.8 copy-start.4
  543.3 59.1 %copy-start.6 = (f32[2,76,304]{2,0,1:T(2,128)S(1)}, f32[2,76,304]{2,0,1:T(2,128)}, u32[]{:S(2)}) copy-start(f32[2,76,304]{2,0,1:T(2,128)} %param.38) | copy-start | bytes 554500
